TPU v7x, 32 devices: a whole 2x2x4 slice. The times are simulated.
32 devices in a mesh: grp: 4 (over y, x), tile: 8 (over z, core).
Axes of the slice: x: 2, y: 2, z: 4, core: 2. Of those that a mesh axis runs over, the one named last changes fastest.
Arguments:
- temp: bfloat16 [48, 64, 2048], P(None, 'grp', 'tile'), may hold values from -6 to 6
- humid: bfloat16 [48, 64, 2048], P(None, 'grp', 'tile'), may hold values from -5 to 5
- parent: int32 [64, 2048], P('grp', 'tile'), may hold values from 0 to 8191, as said below
- kabs: float32 [112, 48], replicated, may hold values from 0.003 to 1
- planck: float32 [112], replicated, may hold values from 0.5 to 2
- top_flux: float32 [112], replicated, may hold values from 0 to 2
Outputs:
- temp_next: bfloat16 [48, 64, 2048], P(None, 'grp', 'tile')
Inputs may be any that keep to these rules, and one draw needn't show every extreme that they name: parent // 1024 is the tile index, in the same region, of the device owning that parent column; the fine cells of one device name any one owner at most 1024 times.
All inputs are finite; a program needn't handle non-finite values.
Results may differ from a plain program's by a relative error of at most 0.005.
Values may be sent and summed in bfloat16 or wider, within the bound.
A program may use at most 64 MiB of HBM per device.

v0:
```python
import jax
import jax.numpy as jnp
from jax import lax
from jax.sharding import PartitionSpec as P


def with_halo(cells, sides, width):
    for axis, dim in sides:
        count = lax.axis_size(axis)
        head = lax.slice_in_dim(cells, 0, width, axis=dim)
        tail = lax.slice_in_dim(cells, cells.shape[dim] - width, cells.shape[dim], axis=dim)
        cells = jnp.concatenate(
            [
                lax.ppermute(tail, axis, [(i, (i + 1) % count) for i in range(count)]),
                cells,
                lax.ppermute(head, axis, [((i + 1) % count, i) for i in range(count)]),
            ],
            axis=dim,
        )
    return cells


def recur(coef, source, init):
    levels = coef.shape[0]
    blocks = levels // 8
    rest = coef.shape[1:]
    coef4 = coef.reshape((blocks, 8) + rest)
    source4 = source.reshape((blocks, 8) + rest)
    prod_list = []
    part_list = []
    prod_now = jnp.ones((blocks,) + rest, jnp.float32)
    part_now = jnp.zeros((blocks,) + rest, jnp.float32)
    for inner in range(8):
        prod_now = coef4[:, inner] * prod_now
        part_now = coef4[:, inner] * part_now + source4[:, inner]
        prod_list.append(prod_now)
        part_list.append(part_now)
    starts = []
    carry = init
    for outer in range(blocks):
        starts.append(carry)
        carry = prod_list[7][outer] * carry + part_list[7][outer]
    start = jnp.stack(starts, 0)
    result = jnp.stack([prod_list[j] * start + part_list[j] for j in range(8)], 1)
    return result.reshape((levels,) + rest)


def radiate(tc, hc, kabs, planck, top_flux):
    levels, count = tc.shape
    kblk = kabs.reshape(-1, 16, levels)
    pblk = planck.reshape(-1, 16)
    tblk = top_flux.reshape(-1, 16)
    absorb = jnp.exp(0.5 * hc)[:, None, :]
    emit = jnp.exp(0.25 * tc)[:, None, :]

    def one_block(items):
        k_blk, p_blk, t_blk = items
        tau = jnp.transpose(k_blk)[:, :, None] * absorb
        trans = jnp.exp(-tau)
        source = p_blk[None, :, None] * emit * (1.0 - trans)
        top = jnp.broadcast_to(t_blk[:, None], (16, count))
        down = recur(trans, source, top)
        up = recur(trans[::-1], source[::-1], 0.3 * down[-1])[::-1]
        net = down - up
        top_net = top - up[0]
        before = jnp.concatenate([top_net[None], net[:-1]], 0)
        return jnp.sum(before - net, axis=1)

    parts = lax.map(one_block, (kblk, pblk, tblk))
    return jnp.sum(parts, axis=0) * (levels / kabs.shape[0])


def laplace(padded):
    value = padded.astype(jnp.float32)
    centre = value[:, 1:-1, 1:-1]
    return (
        value[:, :-2, 1:-1]
        + value[:, 2:, 1:-1]
        + value[:, 1:-1, :-2]
        + value[:, 1:-1, 2:]
        - 4.0 * centre
    )


def on_device(temp, humid, parent, kabs, planck, top_flux):
    levels = temp.shape[0]
    fine = temp.shape[1] * temp.shape[2]
    owned = fine // 4
    tiles = lax.axis_size("tile")
    capacity_limit = 2 * fine // tiles
    width = tiles * capacity_limit
    padded = with_halo(temp, (("grp", 1), ("tile", 2)), 1)
    first = (temp.astype(jnp.float32) + 0.2 * laplace(padded)).astype(jnp.bfloat16)
    flat_parent = parent.reshape(-1)
    owner = flat_parent // owned
    local = flat_parent % owned
    onehot = (owner[:, None] == jnp.arange(tiles, dtype=jnp.int32)[None, :]).astype(jnp.int32)
    position = jnp.sum(jnp.cumsum(onehot, axis=0) * onehot, axis=1) - 1
    slot = owner * capacity_limit + position
    values = jnp.concatenate([temp.reshape(levels, fine), humid.reshape(levels, fine)], 0)
    outgoing = jnp.zeros((2 * levels, width), jnp.bfloat16).at[:, slot].set(values)
    labels = jnp.full((1, width), owned, jnp.int32).at[0, slot].set(local)
    incoming, in_labels = (
        lax.all_to_all(outgoing, "tile", split_axis=1, concat_axis=1, tiled=True),
        lax.all_to_all(labels, "tile", split_axis=1, concat_axis=1, tiled=True),
    )
    received = in_labels[0].astype(jnp.int32)
    sums = jax.ops.segment_sum(
        jnp.transpose(incoming.astype(jnp.float32)), received, num_segments=owned
    )
    counts = jax.ops.segment_sum(jnp.ones((width,), jnp.float32), received, num_segments=owned)
    means = sums / jnp.maximum(counts, 1.0)[:, None]
    tc = jnp.transpose(means[:, :levels])
    hc = jnp.transpose(means[:, levels:])
    heat_c = radiate(tc, hc, kabs, planck, top_flux).astype(jnp.bfloat16)
    hmean = hc.astype(jnp.bfloat16)
    answer = jnp.concatenate([heat_c, hmean], 0)[:, jnp.minimum(received, owned - 1)]
    returned = lax.all_to_all(answer, "tile", split_axis=1, concat_axis=1, tiled=True)
    picked = returned[:, slot]
    heat_cell = picked[:levels]
    hmean_cell = picked[levels:]
    heat_f = heat_cell.astype(jnp.float32) + 0.5 * (
        humid.reshape(levels, fine).astype(jnp.float32) - hmean_cell.astype(jnp.float32)
    )
    second = (first.astype(jnp.float32) + 0.5 * heat_f.reshape(temp.shape)).astype(jnp.bfloat16)
    padded_second = with_halo(second, (("grp", 1), ("tile", 2)), 1)
    return (second.astype(jnp.float32) + 0.2 * laplace(padded_second)).astype(jnp.bfloat16)


def solution(mesh):
    return jax.shard_map(
        on_device,
        mesh=mesh,
        in_specs=(P(None, "grp", "tile"), P(None, "grp", "tile"), P("grp", "tile"), P(), P(), P()),
        out_specs=P(None, "grp", "tile"),
        check_vma=False,
    )
```

profile of v0, /device:TPU:0, one launch (start us, length us, event | category | flops | bytes accessed | tf_op | source)
XLA Modules:
  0.0 444.1 jit_solution(5493296953877921672)
XLA Ops:
  0.8 2.3 reduce-window.6
  7.1 16.1 %scatter_custom_fusion.3 = s32[8192]{0:T(1024)} fusion(s32[4096]{0:T(1024)S(1)} %broadcast_select_fusion, s32[4096]{0:T(1024)S(1)} %get-tuple-element.125, s32[]{:T(128)} %constant.40.clone.1), kind=kCustom, calls=%fused_computation.230 | custom fusion | bytes 32772
  23.2 6.4 %all-to-all-start = ((s32[1,8,1024]{2,0,1:T(1,128)}), s32[1,8,1024]{2,0,1:T(1,128)S(1)}, u32[]{:S(2)}, u32[]{:S(2)}) async-start(s32[1,8,1024]{2,0,1:T(1,128)} %bitcast.87), calls=%async_computation | async-start | bytes 65536 | tf_op jit(solution)/shard_map/all_to_all | solution.py:105
  32.6 12.8 %scatter_custom_fusion = bf16[96,8192]{0,1:T(8,128)(2,1)S(1)} fusion(s32[4096]{0:T(1024)S(1)} %bitcast.628, bf16[48,4096]{0,1:T(8,128)(2,1)S(1)} %bitcast.621, bf16[]{:T(256)} %constant.105, bf16[48,4096]{0,1:T(8,128)(2,1)} %bitcast.627, bf16[]{:T(256)} %constant.80.clone.1), kind=kCustom, calls=%fused_computation.165 | custom fusion | flops 1572864 | bytes 3014660 | tf_op jit(solution)/shard_map/scatter | solution.py:101
  45.4 2.5 copy.300
  47.9 5.1 %all-to-all-start.1 = ((bf16[96,8,1024]{2,0,1:T(8,128)(2,1)}), bf16[96,8,1024]{2,0,1:T(8,128)(2,1)S(1)}, u32[]{:S(2)}, u32[]{:S(2)}) async-start(bf16[96,8,1024]{2,0,1:T(8,128)(2,1)} %copy.300), calls=%async_computation.1 | async-start | bytes 3145728 | tf_op jit(solution)/shard_map/all_to_all | solution.py:104
  53.3 48.3 %scatter_custom_fusion.2 = f32[1024]{0:T(1024)S(1)} fusion(s32[8192]{0:T(1024)S(1)} %bitcast.633, f32[8192]{0:T(1024)S(1)} %broadcast.269, f32[]{:T(128)} %constant.39.clone.1), kind=kCustom, calls=%fused_computation.241 | custom fusion | flops 8192 | bytes 4100 | tf_op jit(solution)/shard_map/scatter-add | solution.py:111
  102.9 3.3 copy.302
  106.3 44.6 %scatter_custom_fusion.1 = f32[1024,96]{1,0:T(8,128)S(1)} fusion(s32[8192]{0:T(1024)S(1)} %bitcast.634, f32[8192,96]{1,0:T(8,128)} %copy.302, f32[]{:T(128)} %constant.39.clone.1), kind=kCustom, calls=%fused_computation.190 | custom fusion | flops 786432 | bytes 393728 | tf_op jit(solution)/shard_map/scatter-add | solution.py:108
  151.8 159.8 %while.10 = (s32[]{:T(128)}, f32[7,48,1024]{2,1,0:T(8,128)}, f32[7,16]{1,0:T(8,128)S(1)}, f32[7,16,48]{2,1,0:T(8,128)S(1)}, f32[48,1,1024]{2,0,1:T(8,128)S(1)}, ...) while((s32[]{:T(128)}, f32[7,48,1024]{2,1,0:T(8,128)}, f32[7,16]{1,0:T(8,128)S(1)}, ...), condition=%wide.region_9.10_spmd, body=%wide.region_7.9_spmd.sunk | while | flops 26214400 | bytes 160786352 | solution.py:69
  156.0 1.6 copy-done.1
  157.6 3.5 negate_exponential_fusion.5
  161.1 1.9 rev.14
  163.0 2.1 rev.15
  165.1 2.6 bitcast_add_fusion.22
  178.8 1.6 copy-done.1
  180.5 3.5 negate_exponential_fusion.5
  183.9 1.9 rev.14
  185.8 2.1 rev.15
  187.9 2.6 bitcast_add_fusion.22
  201.7 1.6 copy-done.1
  203.3 3.5 negate_exponential_fusion.5
  206.7 1.9 rev.14
  208.7 2.1 rev.15
  210.8 2.6 bitcast_add_fusion.22
  226.1 3.5 negate_exponential_fusion.5
  229.6 1.9 rev.14
  231.5 2.1 rev.15
  233.6 2.6 bitcast_add_fusion.22
  247.3 1.6 copy-done.1
  248.9 3.5 negate_exponential_fusion.5
  252.4 1.9 rev.14
  254.3 2.1 rev.15
  256.4 2.6 bitcast_add_fusion.22
  270.1 1.6 copy-done.1
  271.8 3.5 negate_exponential_fusion.5
  275.2 1.9 rev.14
  277.1 2.1 rev.15
  279.3 2.6 bitcast_add_fusion.22
  294.6 3.5 negate_exponential_fusion.5
  298.1 1.9 rev.14
  300.0 2.1 rev.15
  302.1 2.6 bitcast_add_fusion.22
  314.2 28.0 %gather_fusion = bf16[8192,96]{1,0:T(8,128)(2,1)S(1)} fusion(bf16[96,1024]{0,1:T(8,128)(2,1)S(1)} %copy.304, s32[8192]{0:T(1024)} %broadcast_clamp_fusion), kind=kCustom, calls=%fused_computation | custom fusion | bytes 3178496 | tf_op jit(solution)/shard_map/gather | solution.py:117
  342.2 2.5 copy.305
  344.7 13.0 %all-to-all-start.2 = ((bf16[96,8,1024]{2,0,1:T(8,128)(2,1)}), bf16[96,8,1024]{2,0,1:T(8,128)(2,1)}, u32[]{:S(2)}, u32[]{:S(2)}) async-start(bf16[96,8,1024]{2,0,1:T(8,128)(2,1)} %copy.305), calls=%async_computation.2 | async-start | bytes 3145728 | tf_op jit(solution)/shard_map/all_to_all | solution.py:118
  357.8 3.1 collective-permute-start.1
  360.9 2.1 collective-permute-done.1
  363.1 2.9 collective-permute-done
  366.4 2.8 collective-permute-start.3
  369.2 21.2 %collective-permute-done.3 = bf16[48,18,1]{2,1,0:T(8,128)(2,1)S(1)} collective-permute-done((bf16[48,18,1]{2,1,0:T(8,128)(2,1)S(1)}, bf16[48,18,1]{2,1,0:T(8,128)(2,1)S(1)}, u32[]{:S(2)}, u32[]{:S(2)}) %collective-permute-start.3) | collective-permute-done | bytes 1760 | tf_op jit(solution)/shard_map/ppermute | solution.py:16
  390.5 3.4 collective-permute-done.2
  393.8 2.1 maximum_convert_fusion
  395.9 2.9 all-to-all-done.2
  398.8 2.9 copy.306
  401.7 14.9 %gather_fusion.1 = bf16[4096,96]{1,0:T(8,128)(2,1)} fusion(bf16[96,8192]{0,1:T(8,128)(2,1)S(1)} %bitcast.615, s32[4096]{0:T(1024)S(1)} %broadcast_clamp_fusion.1), kind=kCustom, calls=%fused_computation.1 | custom fusion | bytes 1589248 | tf_op jit(solution)/shard_map/gather | solution.py:119
  416.6 3.7 add_multiply_fusion
  420.3 2.4 copy.307
  423.7 3.1 collective-permute-start.5
  426.8 1.7 collective-permute-done.5
  428.5 3.2 collective-permute-done.4
  432.8 6.7 %collective-permute-done.7 = bf16[48,18,1]{2,1,0:T(8,128)(2,1)S(1)} collective-permute-done((bf16[48,18,1]{2,1,0:T(8,128)(2,1)S(1)}, bf16[48,18,1]{2,1,0:T(8,128)(2,1)S(1)}, u32[]{:S(2)}, u32[]{:S(2)}) %collective-permute-start.7) | collective-permute-done | bytes 1760 | tf_op jit(solution)/shard_map/ppermute | solution.py:16
  439.6 2.1 collective-permute-done.6
  442.5 1.6 fusion.49
  (522 shorter events, 95.1 us)
Async XLA Ops:
  0.0 31.1 %copy-start.10 = (bf16[48,16,256]{2,1,0:T(8,128)(2,1)S(1)}, bf16[48,16,256]{2,1,0:T(8,128)(2,1)}, u32[]{:S(2)}) copy-start(bf16[48,16,256]{2,1,0:T(8,128)(2,1)} %param.8) | copy-start | bytes 1179652
  5.5 39.9 %copy-start.14 = (s32[4096,1]{0,1:T(1,128)}, s32[4096,1]{0,1:T(1,128)S(1)}, u32[]{:S(2)}) copy-start(s32[4096,1]{0,1:T(1,128)S(1)} %compare_select_fusion.1) | copy-start | bytes 49156
  23.2 24.8 %all-to-all-start = ((s32[1,8,1024]{2,0,1:T(1,128)}), s32[1,8,1024]{2,0,1:T(1,128)S(1)}, u32[]{:S(2)}, u32[]{:S(2)}) async-start(s32[1,8,1024]{2,0,1:T(1,128)} %bitcast.87), calls=%async_computation | async-start | bytes 65536 | tf_op jit(solution)/shard_map/all_to_all | solution.py:105
  31.1 16.8 %copy-start.8 = (bf16[48,16,256]{0,2,1:T(8,128)(2,1)}, bf16[48,16,256]{0,2,1:T(8,128)(2,1)S(1)}, u32[]{:S(2)}) copy-start(bf16[48,16,256]{0,2,1:T(8,128)(2,1)S(1)} %copy.299) | copy-start | bytes 1179652
  45.4 7.6 %copy-start.19 = (f32[112]{0:T(128)S(1)}, f32[112]{0:T(128)}, u32[]{:S(2)}) copy-start(f32[112]{0:T(128)} %param.13) | copy-start | bytes 1348
  45.4 7.7 %copy-start.18 = (f32[112,48]{0,1:T(8,128)S(1)}, f32[112,48]{0,1:T(8,128)}, u32[]{:S(2)}) copy-start(f32[112,48]{0,1:T(8,128)} %param.11) | copy-start | bytes 64516
  45.4 7.8 %copy-start.20 = (f32[112]{0:T(128)S(1)}, f32[112]{0:T(128)}, u32[]{:S(2)}) copy-start(f32[112]{0:T(128)} %param.12) | copy-start | bytes 1348
  47.9 54.4 %all-to-all-start.1 = ((bf16[96,8,1024]{2,0,1:T(8,128)(2,1)}), bf16[96,8,1024]{2,0,1:T(8,128)(2,1)S(1)}, u32[]{:S(2)}, u32[]{:S(2)}) async-start(bf16[96,8,1024]{2,0,1:T(8,128)(2,1)} %copy.300), calls=%async_computation.1 | async-start | bytes 3145728 | tf_op jit(solution)/shard_map/all_to_all | solution.py:104
  155.5 2.1 copy-start.13
  165.1 2.9 copy-start.2
  167.7 1.9 copy-start
  172.9 1.8 copy-start.4
  172.9 1.8 copy-start.6
  172.9 1.8 copy-start.17
  178.3 2.1 copy-start.13
  187.9 2.9 copy-start.2
  190.6 1.9 copy-start
  195.7 1.8 copy-start.4
  195.7 1.8 copy-start.6
  195.7 1.8 copy-start.17
  201.2 2.1 copy-start.13
  210.8 2.9 copy-start.2
  213.4 1.9 copy-start
  218.6 1.8 copy-start.4
  218.6 1.8 copy-start.6
  218.6 1.8 copy-start.17
  224.0 2.1 copy-start.13
  233.6 2.9 copy-start.2
  236.2 1.9 copy-start
  241.4 1.8 copy-start.4
  241.4 1.8 copy-start.6
  241.4 1.8 copy-start.17
  246.8 2.1 copy-start.13
  256.4 2.9 copy-start.2
  259.0 1.9 copy-start
  264.2 1.8 copy-start.4
  264.2 1.8 copy-start.6
  264.2 1.8 copy-start.17
  269.6 2.1 copy-start.13
  270.1 1.7 copy-start.1
  279.2 2.9 copy-start.2
  281.9 1.9 copy-start
  287.0 1.8 copy-start.4
  287.1 1.8 copy-start.6
  287.1 1.8 copy-start.17
  292.5 2.1 copy-start.13
  302.1 2.9 copy-start.2
  304.7 1.9 copy-start
  309.9 1.8 copy-start.4
  309.9 1.8 copy-start.6
  309.9 1.8 copy-start.17
  342.2 15.5 %copy-start.11 = (bf16[48,16,256]{2,1,0:T(8,128)(2,1)S(1)}, bf16[48,16,256]{2,1,0:T(8,128)(2,1)}, u32[]{:S(2)}) copy-start(bf16[48,16,256]{2,1,0:T(8,128)(2,1)} %param.8) | copy-start | bytes 1179652
  344.7 24.5 %copy-start.15 = (s32[4096,1]{0,1:T(1,128)S(1)}, s32[4096,1]{0,1:T(1,128)}, u32[]{:S(2)}) copy-start(s32[4096,1]{0,1:T(1,128)} %copy-done.14) | copy-start | bytes 49156
  344.7 54.1 %all-to-all-start.2 = ((bf16[96,8,1024]{2,0,1:T(8,128)(2,1)}), bf16[96,8,1024]{2,0,1:T(8,128)(2,1)}, u32[]{:S(2)}, u32[]{:S(2)}) async-start(bf16[96,8,1024]{2,0,1:T(8,128)(2,1)} %copy.305), calls=%async_computation.2 | async-start | bytes 3145728 | tf_op jit(solution)/shard_map/all_to_all | solution.py:118
  357.8 5.3 %collective-permute-start.1 = (bf16[48,1,256]{2,1,0:T(2,128)(2,1)S(1)}, bf16[48,1,256]{2,1,0:T(2,128)(2,1)S(1)}, u32[]{:S(2)}, u32[]{:S(2)}) collective-permute-start(bf16[48,1,256]{2,1,0:T(2,128)(2,1)S(1)} %get-tuple-element.122), channel_id=1, source_target_pairs={{8,0},{16,8},{24,16},{0,24},{9,1},{17,9},{25,17},{1,25},{10,2},{18... | collective-permute-start | bytes 73736 | tf_op jit(solution)/shard_map/ppermute | solution.py:16
  360.9 5.0 %collective-permute-start = (bf16[48,1,256]{2,1,0:T(2,128)(2,1)S(1)}, bf16[48,1,256]{2,1,0:T(2,128)(2,1)S(1)}, u32[]{:S(2)}, u32[]{:S(2)}) collective-permute-start(bf16[48,1,256]{2,1,0:T(2,128)(2,1)S(1)} %get-tuple-element.121), channel_id=1, source_target_pairs={{0,8},{8,16},{16,24},{24,0},{1,9},{9,17},{17,25},{25,1},{2,10},{10... | collective-permute-start | bytes 73736 | tf_op jit(solution)/shard_map/ppermute | solution.py:14
  366.4 24.0 %collective-permute-start.3 = (bf16[48,18,1]{2,1,0:T(8,128)(2,1)S(1)}, bf16[48,18,1]{2,1,0:T(8,128)(2,1)S(1)}, u32[]{:S(2)}, u32[]{:S(2)}) collective-permute-start(bf16[48,18,1]{2,1,0:T(8,128)(2,1)S(1)} %get-tuple-element.118), channel_id=1, source_target_pairs={{1,0},{2,1},{3,2},{4,3},{5,4},{6,5},{7,6},{0,7},{9,8},{10,9},{11,1... | collective-permute-start | bytes 5192 | tf_op jit(solution)/shard_map/ppermute | solution.py:16
  369.2 24.6 %collective-permute-start.2 = (bf16[48,18,1]{2,1,0:T(8,128)(2,1)S(1)}, bf16[48,18,1]{2,1,0:T(8,128)(2,1)S(1)}, u32[]{:S(2)}, u32[]{:S(2)}) collective-permute-start(bf16[48,18,1]{2,1,0:T(8,128)(2,1)S(1)} %get-tuple-element.117), channel_id=1, source_target_pairs={{0,1},{1,2},{2,3},{3,4},{4,5},{5,6},{6,7},{7,0},{8,9},{9,10},{10,1... | collective-permute-start | bytes 5192 | tf_op jit(solution)/shard_map/ppermute | solution.py:14
  401.7 14.9 %copy-start.9 = (bf16[48,16,256]{0,2,1:T(8,128)(2,1)S(1)}, bf16[48,16,256]{0,2,1:T(8,128)(2,1)}, u32[]{:S(2)}) copy-start(bf16[48,16,256]{0,2,1:T(8,128)(2,1)} %copy-done.8) | copy-start | bytes 1179652
  416.6 6.0 %copy-start.7 = (f32[48,18,258]{2,1,0:T(8,128)S(1)}, f32[48,18,258]{2,1,0:T(8,128)}, u32[]{:S(2)}) copy-start(f32[48,18,258]{2,1,0:T(8,128)} %maximum_convert_fusion) | copy-start | bytes 2674948
  423.7 4.9 %collective-permute-start.5 = (bf16[48,1,256]{2,1,0:T(2,128)(2,1)S(1)}, bf16[48,1,256]{2,1,0:T(2,128)(2,1)S(1)}, u32[]{:S(2)}, u32[]{:S(2)}) collective-permute-start(bf16[48,1,256]{2,1,0:T(2,128)(2,1)S(1)} %get-tuple-element.120), channel_id=1, source_target_pairs={{8,0},{16,8},{24,16},{0,24},{9,1},{17,9},{25,17},{1,25},{10,2},{18... | collective-permute-start | bytes 73736 | tf_op jit(solution)/shard_map/ppermute | solution.py:16
  426.8 5.0 %collective-permute-start.4 = (bf16[48,1,256]{2,1,0:T(2,128)(2,1)S(1)}, bf16[48,1,256]{2,1,0:T(2,128)(2,1)S(1)}, u32[]{:S(2)}, u32[]{:S(2)}) collective-permute-start(bf16[48,1,256]{2,1,0:T(2,128)(2,1)S(1)} %get-tuple-element.119), channel_id=1, source_target_pairs={{0,8},{8,16},{16,24},{24,0},{1,9},{9,17},{17,25},{25,1},{2,10},{10... | collective-permute-start | bytes 73736 | tf_op jit(solution)/shard_map/ppermute | solution.py:14
  432.3 7.3 %collective-permute-start.7 = (bf16[48,18,1]{2,1,0:T(8,128)(2,1)S(1)}, bf16[48,18,1]{2,1,0:T(8,128)(2,1)S(1)}, u32[]{:S(2)}, u32[]{:S(2)}) collective-permute-start(bf16[48,18,1]{2,1,0:T(8,128)(2,1)S(1)} %get-tuple-element.116), channel_id=1, source_target_pairs={{1,0},{2,1},{3,2},{4,3},{5,4},{6,5},{7,6},{0,7},{9,8},{10,9},{11,1... | collective-permute-start | bytes 5192 | tf_op jit(solution)/shard_map/ppermute | solution.py:16
  432.3 9.3 %collective-permute-start.6 = (bf16[48,18,1]{2,1,0:T(8,128)(2,1)S(1)}, bf16[48,18,1]{2,1,0:T(8,128)(2,1)S(1)}, u32[]{:S(2)}, u32[]{:S(2)}) collective-permute-start(bf16[48,18,1]{2,1,0:T(8,128)(2,1)S(1)} %get-tuple-element.115), channel_id=1, source_target_pairs={{0,1},{1,2},{2,3},{3,4},{4,5},{5,6},{6,7},{7,0},{8,9},{9,10},{10,1... | collective-permute-start | bytes 5192 | tf_op jit(solution)/shard_map/ppermute | solution.py:14
  (34 other events, 41.9 us)
where the time goes:
time: 447 us; the launch traced here: 444 us
  other arithmetic  220 us (49%)
  local copies, waits for them, and re-layouts  141 us (32%)
  waiting for transfers between devices  46.2 us (10%)
  starting transfers between devices  34 us (8%)
    scatter-add x1, other arithmetic, on_device(): jax.ops.segment_sum(jnp.ones((width,), jnp.float32), received, num_segmen...  48.3 us
    scatter-add x1, other arithmetic, on_device(): jax.ops.segment_sum(jnp.transpose(incoming.astype(jnp.float32)), received...  44.6 us
    ppermute x4, waiting for transfers between devices, with_halo(): lax.ppermute(head, axis, [((i + 1) % count, i) for i in range(count)])  31.8 us
    exp x14, other arithmetic, one_block(): trans = jnp.exp(-tau)  29.3 us
    rev x14, local copies, waits for them, and re-layouts, one_block(): up = recur(trans[::-1], source[::-1], 0.3 * down[-1])[::-1]  28.1 us
    gather x1, local copies, waits for them, and re-layouts, on_device(): jnp.concatenate([heat_c, hmean], 0)[:, jnp.minimum(received, owned - 1)]  28 us
    while x161, local copies, waits for them, and re-layouts  22.7 us
    add x14, other arithmetic, recur(): part_now = coef4[:, inner] * part_now + source4[:, inner]  22.7 us
  transfers between devices with their start and end apart: 11, of which 9 were waited for; matrix products, arithmetic and copies ran while one was open for 16% of the time, Pallas kernels for 0%

commit v1 on v0

v1 whole, which is shorter than its diff:
```python
import functools
import math

import jax
import jax.numpy as jnp
from jax import lax
from jax.experimental import pallas as pl
from jax.experimental.pallas import tpu as pltpu
from jax.sharding import PartitionSpec as P

F32 = jnp.float32
BF16 = jnp.bfloat16
VMEM_LIMIT = 60 * 1024 * 1024
VSPEC = pl.BlockSpec(memory_space=pltpu.VMEM)


def partial_kernel(chunks, vals_ref, parent_ref, out_ref, onehot, masked):
    rows, feats, lanes = vals_ref.shape
    owner = pl.program_id(0)

    @pl.when(owner == 0)
    def _():
        lo_iota = lax.broadcasted_iota(jnp.int32, (lanes, lanes), 0)
        for r in range(rows):
            low = parent_ref[r : r + 1, :] % lanes
            onehot[:, r * lanes : (r + 1) * lanes] = (lo_iota == low).astype(F32).astype(BF16)

    for r in range(rows):
        high = jnp.broadcast_to(parent_ref[r : r + 1, :] // lanes, (16, lanes))
        for c in range(chunks):
            mask = (high == owner * chunks + c).astype(F32).astype(BF16)
            for v in range(feats // 16):
                at = c * feats + v * 16
                masked[at : at + 16, r * lanes : (r + 1) * lanes] = (
                    vals_ref[r, v * 16 : (v + 1) * 16, :] * mask
                )
    total = lax.dot_general(
        masked[...], onehot[...], (((1,), (1,)), ((), ())), preferred_element_type=F32
    )
    out_ref[0] = total.astype(BF16)
    for c in range(chunks):
        at = slice((c + 1) * feats - 16, (c + 1) * feats)
        count = total[at]
        high = jnp.floor(count * (1.0 / 32.0))
        row = lax.broadcasted_iota(jnp.int32, count.shape, 0)
        out_ref[0, at, :] = jnp.where(row == 0, high, count - 32.0 * high).astype(BF16)


def radiate_kernel(levels, feats, recv_ref, kabs_ref, planck_ref, top_ref, out_ref, sums, absorb, emit, trans, net, heat):
    tiles = recv_ref.shape[0]
    lanes = recv_ref.shape[2]
    chunks = recv_ref.shape[1] // feats
    octets = kabs_ref.shape[1] // 8
    group = octets // 2 if octets % 2 == 0 else octets
    width = 128

    def add(i, carry):
        at = pl.ds(pl.multiple_of(i * 16, 16), 16)
        acc = recv_ref[0, at, :].astype(F32)
        for s in range(1, tiles):
            acc = acc + recv_ref[s, at, :].astype(F32)
        sums[at, :] = acc
        return carry

    lax.fori_loop(0, chunks * feats // 16, add, 0)
    for c in range(chunks):
        base = c * feats
        cnt = sums[base + 2 * levels : base + 2 * levels + 1, :] * 32.0
        cnt = cnt + sums[base + 2 * levels + 1 : base + 2 * levels + 2, :]
        cnt = jnp.maximum(cnt, 1.0)
        for j in range(lanes // width):
            part = slice(j * width, (j + 1) * width)
            ct = c * (lanes // width) + j
            tc = sums[base : base + levels, part] / cnt[:, part]
            hc = sums[base + levels : base + 2 * levels, part] / cnt[:, part]
            emit[ct] = jnp.exp(0.25 * tc)
            absorb[ct] = jnp.exp(0.5 * hc) * (-math.log2(math.e))
            heat[ct] = -0.5 * hc

    scale = levels / (octets * 8)

    def column(ct, carry):
        for half in range(octets // group):
            gs = [(half * group + p) * 8 for p in range(group)]
            planck = [planck_ref[g : g + 8, :] for g in gs]
            down = [top_ref[g : g + 8, :] for g in gs]
            if half == 0:
                before = sum(down[1:], down[0])
                net[0] = before
            else:
                net[0] = net[0] + sum(down[1:], down[0])
            for k in range(levels):
                ab = absorb[ct, k : k + 1, :]
                em = emit[ct, k : k + 1, :]
                acc = None
                for p in range(group):
                    t = jnp.exp2(kabs_ref[k, gs[p] : gs[p] + 8, :] * ab)
                    trans[k, p] = t
                    s = planck[p] * em
                    down[p] = s + t * (down[p] - s)
                    acc = down[p] if acc is None else acc + down[p]
                net[k + 1] = acc if half == 0 else net[k + 1] + acc
            up = [0.3 * d for d in down]
            for k in range(levels - 1, -1, -1):
                em = emit[ct, k : k + 1, :]
                acc = None
                for p in range(group):
                    s = planck[p] * em
                    up[p] = s + trans[k, p] * (up[p] - s)
                    acc = up[p] if acc is None else acc + up[p]
                net[k + 1] = net[k + 1] - acc
            net[0] = net[0] - acc
        for k in range(levels):
            row = jnp.sum(net[k] - net[k + 1], axis=0, keepdims=True) * scale
            heat[ct, k : k + 1, :] = heat[ct, k : k + 1, :] + row
        return carry

    lax.fori_loop(0, chunks * lanes // width, column, 0)
    per = lanes // width
    for c in range(chunks):
        for j in range(per):
            out_ref[c * levels : (c + 1) * levels, j * width : (j + 1) * width] = heat[c * per + j].astype(BF16)


def laplace_row(centre, above, below, left, right):
    lanes = centre.shape[1]
    lane = lax.broadcasted_iota(jnp.int32, centre.shape, 1)
    west = jnp.where(lane == 0, left, pltpu.roll(centre, 1, 1))
    east = jnp.where(lane == lanes - 1, right, pltpu.roll(centre, lanes - 1, 1))
    return above + below + west + east - 4.0 * centre


def gather_kernel(levels, table_ref, parent_ref, temp_ref, humid_ref, up_ref, dn_ref, lf_ref, rt_ref, out_ref):
    rows, _, lanes = temp_ref.shape
    tiles = table_ref.shape[0]
    chunks = table_ref.shape[1] // levels
    lo_iota = lax.broadcasted_iota(jnp.int32, (lanes, lanes), 0)
    for r in range(rows):
        low = parent_ref[r : r + 1, :] % lanes
        high = jnp.broadcast_to(parent_ref[r : r + 1, :] // lanes, (levels, lanes))
        onehot = (lo_iota == low).astype(F32).astype(BF16)

        def owner(i, acc):
            span = 4
            got = jnp.dot(
                table_ref[pl.ds(i * span, span)].reshape(span * chunks * levels, lanes),
                onehot,
                preferred_element_type=F32,
            )
            for c in range(span * chunks):
                acc = jnp.where(high == i * span * chunks + c, got[c * levels : (c + 1) * levels], acc)
            return acc

        picked = lax.fori_loop(0, tiles // 4, owner, jnp.zeros((levels, lanes), F32))
        centre = temp_ref[r].astype(F32)
        above = (temp_ref[r - 1] if r > 0 else up_ref[0]).astype(F32)
        below = (temp_ref[r + 1] if r < rows - 1 else dn_ref[0]).astype(F32)
        lap = laplace_row(centre, above, below, lf_ref[:, r : r + 1], rt_ref[:, r : r + 1])
        first = (centre + 0.2 * lap).astype(BF16).astype(F32)
        heat_f = picked + 0.5 * humid_ref[r].astype(F32)
        out_ref[r] = (first + 0.5 * heat_f).astype(BF16)


def laplace_kernel(x_ref, up_ref, dn_ref, lf_ref, rt_ref, out_ref):
    rows = x_ref.shape[0]
    for r in range(rows):
        centre = x_ref[r].astype(F32)
        above = (x_ref[r - 1] if r > 0 else up_ref[0]).astype(F32)
        below = (x_ref[r + 1] if r < rows - 1 else dn_ref[0]).astype(F32)
        lap = laplace_row(centre, above, below, lf_ref[:, r : r + 1], rt_ref[:, r : r + 1])
        out_ref[r] = (centre + 0.2 * lap).astype(BF16)


def halos(x):
    g, t = lax.axis_size("grp"), lax.axis_size("tile")
    ahead = lambda n: [(i, (i + 1) % n) for i in range(n)]
    back = lambda n: [((i + 1) % n, i) for i in range(n)]
    up = lax.ppermute(x[-1:], "grp", ahead(g))
    dn = lax.ppermute(x[:1], "grp", back(g))
    lf = lax.ppermute(jnp.transpose(x[:, :, -1]), "tile", ahead(t)).astype(F32)
    rt = lax.ppermute(jnp.transpose(x[:, :, 0]), "tile", back(t)).astype(F32)
    return up, dn, lf, rt


def on_device(temp, humid, parent, kabs, planck, top_flux):
    levels, rows, lanes = temp.shape
    tiles = lax.axis_size("tile")
    owned = rows * lanes // 4
    chunks = owned // lanes
    feats = 2 * levels + 16
    gpts = kabs.shape[0]
    params = pltpu.CompilerParams(vmem_limit_bytes=VMEM_LIMIT)

    x = jnp.transpose(temp, (1, 0, 2))
    h = jnp.transpose(humid, (1, 0, 2))
    ones = jnp.ones((rows, 16, lanes), BF16)
    vals = jnp.concatenate([x, h, ones], 1)
    partial = pl.pallas_call(
        functools.partial(partial_kernel, chunks),
        out_shape=jax.ShapeDtypeStruct((tiles, chunks * feats, lanes), BF16),
        grid=(tiles,),
        in_specs=[
            pl.BlockSpec((rows, feats, lanes), lambda i: (0, 0, 0)),
            pl.BlockSpec((rows, lanes), lambda i: (0, 0)),
        ],
        out_specs=pl.BlockSpec((1, chunks * feats, lanes), lambda i: (i, 0, 0)),
        scratch_shapes=[
            pltpu.VMEM((lanes, rows * lanes), BF16),
            pltpu.VMEM((chunks * feats, rows * lanes), BF16),
        ],
        compiler_params=params,
    )(vals, parent)
    recv = lax.all_to_all(partial, "tile", split_axis=0, concat_axis=0, tiled=True)

    kb = jnp.broadcast_to(jnp.transpose(kabs)[:, :, None], (levels, gpts, 128))
    pb = jnp.broadcast_to(planck[:, None], (gpts, 128))
    tb = jnp.broadcast_to(top_flux[:, None], (gpts, 128))
    ctiles = owned // 128
    octets = gpts // 8
    group = octets // 2 if octets % 2 == 0 else octets
    table = pl.pallas_call(
        functools.partial(radiate_kernel, levels, feats),
        out_shape=jax.ShapeDtypeStruct((chunks * levels, lanes), BF16),
        in_specs=[VSPEC] * 4,
        out_specs=VSPEC,
        scratch_shapes=[
            pltpu.VMEM((chunks * feats, lanes), F32),
            pltpu.VMEM((ctiles, levels, 128), F32),
            pltpu.VMEM((ctiles, levels, 128), F32),
            pltpu.VMEM((levels, group, 8, 128), F32),
            pltpu.VMEM((levels + 1, 8, 128), F32),
            pltpu.VMEM((ctiles, levels, 128), F32),
        ],
        compiler_params=params,
    )(recv, kb, pb, tb)
    tables = lax.all_gather(table, "tile", axis=0)

    second = pl.pallas_call(
        functools.partial(gather_kernel, levels),
        out_shape=jax.ShapeDtypeStruct((rows, levels, lanes), BF16),
        in_specs=[VSPEC] * 8,
        out_specs=VSPEC,
        compiler_params=params,
    )(tables, parent, x, h, *halos(x))
    out = pl.pallas_call(
        laplace_kernel,
        out_shape=jax.ShapeDtypeStruct((rows, levels, lanes), BF16),
        in_specs=[VSPEC] * 5,
        out_specs=VSPEC,
        compiler_params=params,
    )(second, *halos(second))
    return jnp.transpose(out, (1, 0, 2))


def solution(mesh):
    return jax.shard_map(
        on_device,
        mesh=mesh,
        in_specs=(P(None, "grp", "tile"), P(None, "grp", "tile"), P("grp", "tile"), P(), P(), P()),
        out_specs=P(None, "grp", "tile"),
        check_vma=False,
    )
```

time: 447 us -> 130 us (0.29)
  other arithmetic: 220 us -> 3.74 us
  local copies, waits for them, and re-layouts: 141 us -> 27.1 us
  Pallas kernels: 0 us -> 39.8 us
  waiting for transfers between devices: 46.2 us -> 22.5 us
  blocking collectives: 0 us -> 16.8 us
  starting transfers between devices: 34 us -> 19.5 us
    scatter-add x2 -> x0, other arithmetic: 92.9 us -> none  [the longest x1 48.3 us: on_device(): jax.ops.segment_sum(jnp.ones((width,), jnp.float32), received, num_segmen...]
    gather x2 -> x0, local copies, waits for them, and re-layouts: 42.8 us -> none  [the longest x1 28 us: on_device(): jnp.concatenate([heat_c, hmean], 0)[:, jnp.minimum(received, owned - 1)]]
    pallas_call x0 -> x4, Pallas kernels: none -> 39.8 us  [the longest x1 13 us: on_device(): pl.pallas_call(functools.partial(radiate_kernel, levels, feats), out_shap...]
    exp x14 -> x0, other arithmetic: 29.3 us -> none  [one_block(): trans = jnp.exp(-tau)]
    ppermute x8, waiting for transfers between devices: 43.4 us -> 14.4 us  [the longest x2 14.4 us: halos(): lf = lax.ppermute(jnp.transpose(x[:, :, -1]), 'tile', ahead(t)).astype(F32)]
    rev x14 -> x0, local copies, waits for them, and re-layouts: 28.1 us -> none  [one_block(): up = recur(trans[::-1], source[::-1], 0.3 * down[-1])[::-1]]
    while x161 -> x0, local copies, waits for them, and re-layouts: 22.7 us -> none
    add x14 -> x0, other arithmetic: 22.7 us -> none  [recur(): part_now = coef4[:, inner] * part_now + source4[:, inner]]
  transfers between devices with their start and end apart: 11 -> 9, of which waited for: 9 -> 3; matrix products, arithmetic and copies ran while one was open for 16% -> 17% of each run, Pallas kernels for 0% -> 10%
where the time goes in v1:
time: 130 us
  Pallas kernels  39.8 us (31%)
  local copies, waits for them, and re-layouts  27.1 us (21%)
  waiting for transfers between devices  22.5 us (17%)
  starting transfers between devices  19.5 us (15%)
  blocking collectives  16.8 us (13%)
  other arithmetic  3.74 us (3%)
    all_gather x1, blocking collectives, on_device(): tables = lax.all_gather(table, 'tile', axis=0)  16.8 us
    ppermute x2, waiting for transfers between devices, halos(): lf = lax.ppermute(jnp.transpose(x[:, :, -1]), 'tile', ahead(t)).astype(F32)  14.4 us
    pallas_call x1, Pallas kernels, on_device(): pl.pallas_call(functools.partial(radiate_kernel, levels, feats), out_shap...  13 us
    pallas_call x1, Pallas kernels, on_device(): pl.pallas_call(functools.partial(gather_kernel, levels), out_shape=jax.Sh...  12.8 us
    pallas_call x1, Pallas kernels, on_device(): pl.pallas_call(functools.partial(partial_kernel, chunks), out_shape=jax.S...  11.7 us
    all_to_all x1, waiting for transfers between devices, on_device(): lax.all_to_all(partial, 'tile', split_axis=0, concat_axis=0, tiled=True)  8.1 us
    slice x3, local copies, waits for them, and re-layouts, halos(): dn = lax.ppermute(x[:1], 'grp', back(g))  7.37 us
    unnamed x26, local copies, waits for them, and re-layouts  7.29 us
  transfers between devices with their start and end apart: 9, of which 3 were waited for; matrix products, arithmetic and copies ran while one was open for 17% of the time, Pallas kernels for 10%

profile of v1, /device:TPU:0, one launch (start us, length us, event | category | flops | bytes accessed | tf_op | source)
XLA Modules:
  0.0 129.6 jit_solution(2152342443151618689)
XLA Ops:
  0.0 1.1 copy.30
  1.1 0.0 copy-start.1
  1.1 1.3 copy.19.temp_ref
  2.4 0.0 copy-start.2
  2.4 0.1 pad.2.clone
  2.5 0.6 copy-done.2
  3.1 1.3 maximum_maximum_fusion.vals_ref
  4.4 0.0 copy-start.3
  4.4 11.7 %shard_map.64 = bf16[8,448,256]{2,1,0:T(8,128)(2,1)} custom-call(bf16[16,112,256]{2,1,0:T(8,128)(2,1)} %maximum_maximum_fusion.vals_ref, s32[16,256]{1,0:T(8,128)} %parent_ref.3), custom_call_target="tpu_custom_call" | custom-call | tf_op jit(solution)/shard_map/pallas_call | solution.py:198
  16.1 0.0 copy-done.1
  16.1 6.4 %all-to-all-start = ((bf16[8,448,256]{2,1,0:T(8,128)(2,1)}), bf16[8,448,256]{2,1,0:T(8,128)(2,1)}, u32[]{:S(2)}, u32[]{:S(2)}) async-start(bf16[8,448,256]{2,1,0:T(8,128)(2,1)} %shard_map.64), calls=%async_computation | async-start | bytes 3670016 | tf_op jit(solution)/shard_map/all_to_all | solution.py:213
  22.4 0.0 copy-done.3
  22.4 2.9 %copy.17 = bf16[48,16,256]{1,0,2:T(8,128)(2,1)S(1)} copy(bf16[48,16,256]{2,1,0:T(8,128)(2,1)S(1)} %copy-done.3) | data formatting | bytes 786432 | tf_op args[0]
  25.4 0.5 collective-permute-start.2
  25.9 3.1 %collective-permute-start.3 = (bf16[48,16]{1,0:T(8,128)(2,1)S(1)}, bf16[48,16]{1,0:T(8,128)(2,1)S(1)}, u32[]{:S(2)}, u32[]{:S(2)}) collective-permute-start(bf16[48,16]{1,0:T(8,128)(2,1)S(1)} %get-tuple-element.5), channel_id=1, source_target_pairs={{1,0},{2,1},{3,2},{4,3},{5,4},{6,5},{7,6},{0,7},{9,8},{10,9},{11,1... | collective-permute-start | bytes 4616 | tf_op jit(solution)/shard_map/ppermute | solution.py:181
  29.0 4.0 %fusion = (bf16[1,48,256]{0,1,2:T(8,128)(2,1)}, bf16[1,48,256]{0,1,2:T(8,128)(2,1)}) fusion(bf16[16,48,256]{0,1,2:T(8,128)(2,1)S(1)} %bitcast.23), kind=kLoop, calls=%fused_computation.4 | loop fusion | bytes 98304 | tf_op jit(solution)/shard_map/slice | solution.py:179
  33.1 0.0 copy-start
  33.1 0.0 copy-start.4
  33.1 4.7 %copy.20 = bf16[1,48,256]{2,1,0:T(8,128)(2,1)S(1)} copy(bf16[1,48,256]{0,1,2:T(8,128)(2,1)} %get-tuple-element.8) | data formatting | bytes 49152 | tf_op jit(solution)/shard_map/slice | solution.py:178
  37.8 1.5 %collective-permute-start = (bf16[1,48,256]{2,1,0:T(8,128)(2,1)S(1)}, bf16[1,48,256]{2,1,0:T(8,128)(2,1)S(1)}, u32[]{:S(2)}, u32[]{:S(2)}) collective-permute-start(bf16[1,48,256]{2,1,0:T(8,128)(2,1)S(1)} %copy.20), channel_id=1, source_target_pairs={{0,8},{8,16},{16,24},{24,0},{1,9},{9,17},{17,25},{25,1},{2,10},{10... | collective-permute-start | bytes 73736 | tf_op jit(solution)/shard_map/ppermute | solution.py:178
  39.3 0.0 copy-done
  39.3 0.0 copy-start.9
  39.3 0.0 copy-start.10
  39.3 2.6 %copy.21 = bf16[1,48,256]{2,1,0:T(8,128)(2,1)S(1)} copy(bf16[1,48,256]{0,1,2:T(8,128)(2,1)S(1)} %copy-done) | data formatting | bytes 49152 | tf_op jit(solution)/shard_map/slice | solution.py:179
  41.9 1.5 %collective-permute-start.1 = (bf16[1,48,256]{2,1,0:T(8,128)(2,1)S(1)}, bf16[1,48,256]{2,1,0:T(8,128)(2,1)S(1)}, u32[]{:S(2)}, u32[]{:S(2)}) collective-permute-start(bf16[1,48,256]{2,1,0:T(8,128)(2,1)S(1)} %copy.21), channel_id=1, source_target_pairs={{8,0},{16,8},{24,16},{0,24},{9,1},{17,9},{25,17},{1,25},{10,2},{18... | collective-permute-start | bytes 73736 | tf_op jit(solution)/shard_map/ppermute | solution.py:179
  43.4 13.4 %collective-permute-done.2 = bf16[48,16]{1,0:T(8,128)(2,1)S(1)} collective-permute-done((bf16[48,16]{1,0:T(8,128)(2,1)S(1)}, bf16[48,16]{1,0:T(8,128)(2,1)S(1)}, u32[]{:S(2)}, u32[]{:S(2)}) %collective-permute-start.2) | collective-permute-done | bytes 1568 | tf_op jit(solution)/shard_map/ppermute | solution.py:180
  56.8 0.6 convert_element_type.12.lf_ref
  57.4 0.0 collective-permute-done.3
  57.4 0.6 convert_element_type.13.rt_ref
  58.0 8.1 %all-to-all-done.recv_ref = bf16[8,448,256]{2,1,0:T(8,128)(2,1)} async-done(((bf16[8,448,256]{2,1,0:T(8,128)(2,1)}), bf16[8,448,256]{2,1,0:T(8,128)(2,1)}, u32[]{:S(2)}, u32[]{:S(2)}) %all-to-all-start) | async-done | bytes 1835040 | tf_op jit(solution)/shard_map/all_to_all | solution.py:213
  66.1 0.0 copy-done.4
  66.1 2.0 %broadcast_in_dim.9.kabs_ref = f32[48,112,128]{2,1,0:T(8,128)} broadcast(f32[48,112]{1,0:T(8,128)S(1)} %bitcast.29), dimensions={0,1} | broadcast | bytes 2774016 | tf_op jit(solution)/shard_map/broadcast_in_dim | solution.py:215
  68.1 0.0 copy-done.9
  68.1 0.7 broadcast_in_dim.10.planck_ref
  68.8 0.0 copy-done.10
  68.8 0.7 broadcast_in_dim.11.top_ref
  69.5 13.0 %shard_map.65 = bf16[192,256]{1,0:T(8,128)(2,1)} custom-call(bf16[8,448,256]{2,1,0:T(8,128)(2,1)} %all-to-all-done.recv_ref, f32[48,112,128]{2,1,0:T(8,128)} %broadcast_in_dim.9.kabs_ref, f32[112,128]{1,0:T(8,128)} %broadcast_in_dim.10.planck_ref, f32[112,128]{1,0:T(8,128)} %broadcast_in_dim.11.top_ref), custom_call_target="tpu_custom_call" | custom-call | tf_op jit(solution)/shard_map/pallas_call | solution.py:221
  82.5 16.8 %all-gather = bf16[1536,256]{1,0:T(8,128)(2,1)} all-gather(bf16[192,256]{1,0:T(8,128)(2,1)} %shard_map.65), channel_id=2, replica_groups=mesh['grp'=4,'tile'=8] {'tile'}, dimensions={0}, use_global_device_ids=true | all-gather | bytes 884736 | tf_op jit(solution)/shard_map/all_gather | solution.py:236
  99.3 0.0 collective-permute-done.up_ref
  99.3 0.0 copy-start.5
  99.3 0.0 collective-permute-done.1.dn_ref
  99.3 0.0 copy-start.7
  99.4 0.6 copy-done.5
  99.9 0.0 copy-done.7
  100.0 12.8 %shard_map.66.x_ref = bf16[16,48,256]{2,1,0:T(8,128)(2,1)} custom-call(bf16[8,192,256]{2,1,0:T(8,128)(2,1)} %bitcast.26, s32[16,256]{1,0:T(8,128)} %parent_ref.3, bf16[16,48,256]{2,1,0:T(8,128)(2,1)} %copy-done.2, bf16[16,48,256]{2,1,0:T(8,128)(2,1)} %bitcast.25, bf16[1,48,256]{2,1,0:T(8,128)(2,1)} %copy-done.5, bf16[1,48,256]{2,1,0:T(8,128)(2,1)} %copy-done.7, ...), custom_call_target="tpu_custom_call" | custom-call | tf_op jit(solution)/shard_map/pallas_call | solution.py:238
  112.8 0.8 fusion.2
  113.6 1.5 %collective-permute-start.4 = (bf16[1,48,256]{2,1,0:T(8,128)(2,1)S(1)}, bf16[1,48,256]{2,1,0:T(8,128)(2,1)S(1)}, u32[]{:S(2)}, u32[]{:S(2)}) collective-permute-start(bf16[1,48,256]{2,1,0:T(8,128)(2,1)S(1)} %get-tuple-element.12), channel_id=1, source_target_pairs={{0,8},{8,16},{16,24},{24,0},{1,9},{9,17},{17,25},{25,1},{2,10},{10... | collective-permute-start | bytes 73736 | tf_op jit(solution)/shard_map/ppermute | solution.py:178
  115.0 1.4 %collective-permute-start.5 = (bf16[1,48,256]{2,1,0:T(8,128)(2,1)S(1)}, bf16[1,48,256]{2,1,0:T(8,128)(2,1)S(1)}, u32[]{:S(2)}, u32[]{:S(2)}) collective-permute-start(bf16[1,48,256]{2,1,0:T(8,128)(2,1)S(1)} %get-tuple-element.11), channel_id=1, source_target_pairs={{8,0},{16,8},{24,16},{0,24},{9,1},{17,9},{25,17},{1,25},{10,2},{18... | collective-permute-start | bytes 73736 | tf_op jit(solution)/shard_map/ppermute | solution.py:179
  116.5 1.1 fusion.1
  117.6 0.4 copy.27
  118.0 0.0 collective-permute-start.6
  118.0 0.4 copy.28
  118.4 3.5 %collective-permute-start.7 = (bf16[48,16]{1,0:T(8,128)(2,1)S(1)}, bf16[48,16]{1,0:T(8,128)(2,1)S(1)}, u32[]{:S(2)}, u32[]{:S(2)}) collective-permute-start(bf16[48,16]{1,0:T(8,128)(2,1)S(1)} %bitcast.31), channel_id=1, source_target_pairs={{1,0},{2,1},{3,2},{4,3},{5,4},{6,5},{7,6},{0,7},{9,8},{10,9},{11,1... | collective-permute-start | bytes 4616 | tf_op jit(solution)/shard_map/ppermute | solution.py:181
  122.0 1.0 collective-permute-done.6
  122.9 0.6 convert_element_type.14.lf_ref
  123.6 0.0 collective-permute-done.7
  123.6 0.6 convert_element_type.15.rt_ref
  124.2 0.0 collective-permute-done.4.up_ref
  124.2 0.0 copy-start.6
  124.2 0.0 collective-permute-done.5.dn_ref
  124.2 0.6 copy-done.6
  124.8 0.6 copy-done.8
  125.4 2.3 %shard_map.67 = bf16[16,48,256]{2,1,0:T(8,128)(2,1)} custom-call(bf16[16,48,256]{2,1,0:T(8,128)(2,1)} %shard_map.66.x_ref, bf16[1,48,256]{2,1,0:T(8,128)(2,1)} %copy-done.6, bf16[1,48,256]{2,1,0:T(8,128)(2,1)} %copy-done.8, f32[48,16]{1,0:T(8,128)} %convert_element_type.14.lf_ref, f32[48,16]{1,0:T(8,128)} %convert_element_type.15.rt_ref), custom_call_target="tpu_custom_call" | custom-call | tf_op jit(solution)/shard_map/pallas_call | solution.py:245
  127.7 1.9 %copy.25 = bf16[48,16,256]{2,1,0:T(8,128)(2,1)} copy(bf16[48,16,256]{2,0,1:T(8,128)(2,1)} %bitcast.28) | data formatting | bytes 786432 | tf_op jit(solution)/shard_map/transpose | solution.py:252
  (3 shorter events, 0.0 us)
Async XLA Ops:
  1.1 15.0 %copy-start.1 = (bf16[48,16,256]{2,0,1:T(8,128)(2,1)}, bf16[48,16,256]{2,0,1:T(8,128)(2,1)S(1)}, u32[]{:S(2)}) copy-start(bf16[48,16,256]{2,0,1:T(8,128)(2,1)S(1)} %copy.30) | copy-start | bytes 1179652
  2.4 0.7 copy-start.2
  4.4 18.0 %copy-start.3 = (bf16[48,16,256]{2,1,0:T(8,128)(2,1)S(1)}, bf16[48,16,256]{2,1,0:T(8,128)(2,1)}, u32[]{:S(2)}) copy-start(bf16[48,16,256]{2,1,0:T(8,128)(2,1)} %param.6) | copy-start | bytes 1179652
  16.1 50.0 %all-to-all-start = ((bf16[8,448,256]{2,1,0:T(8,128)(2,1)}), bf16[8,448,256]{2,1,0:T(8,128)(2,1)}, u32[]{:S(2)}, u32[]{:S(2)}) async-start(bf16[8,448,256]{2,1,0:T(8,128)(2,1)} %shard_map.64), calls=%async_computation | async-start | bytes 3670016 | tf_op jit(solution)/shard_map/all_to_all | solution.py:213
  25.4 31.4 %collective-permute-start.2 = (bf16[48,16]{1,0:T(8,128)(2,1)S(1)}, bf16[48,16]{1,0:T(8,128)(2,1)S(1)}, u32[]{:S(2)}, u32[]{:S(2)}) collective-permute-start(bf16[48,16]{1,0:T(8,128)(2,1)S(1)} %get-tuple-element.6), channel_id=1, source_target_pairs={{0,1},{1,2},{2,3},{3,4},{4,5},{5,6},{6,7},{7,0},{8,9},{9,10},{10,1... | collective-permute-start | bytes 4616 | tf_op jit(solution)/shard_map/ppermute | solution.py:180
  25.9 31.4 %collective-permute-start.3 = (bf16[48,16]{1,0:T(8,128)(2,1)S(1)}, bf16[48,16]{1,0:T(8,128)(2,1)S(1)}, u32[]{:S(2)}, u32[]{:S(2)}) collective-permute-start(bf16[48,16]{1,0:T(8,128)(2,1)S(1)} %get-tuple-element.5), channel_id=1, source_target_pairs={{1,0},{2,1},{3,2},{4,3},{5,4},{6,5},{7,6},{0,7},{9,8},{10,9},{11,1... | collective-permute-start | bytes 4616 | tf_op jit(solution)/shard_map/ppermute | solution.py:181
  33.1 6.2 %copy-start = (bf16[1,48,256]{0,1,2:T(8,128)(2,1)S(1)}, bf16[1,48,256]{0,1,2:T(8,128)(2,1)}, u32[]{:S(2)}) copy-start(bf16[1,48,256]{0,1,2:T(8,128)(2,1)} %get-tuple-element.7) | copy-start | bytes 73732
  33.1 33.0 %copy-start.4 = (f32[112,48]{0,1:T(8,128)S(1)}, f32[112,48]{0,1:T(8,128)}, u32[]{:S(2)}) copy-start(f32[112,48]{0,1:T(8,128)} %param.9) | copy-start | bytes 64516
  37.8 61.5 %collective-permute-start = (bf16[1,48,256]{2,1,0:T(8,128)(2,1)S(1)}, bf16[1,48,256]{2,1,0:T(8,128)(2,1)S(1)}, u32[]{:S(2)}, u32[]{:S(2)}) collective-permute-start(bf16[1,48,256]{2,1,0:T(8,128)(2,1)S(1)} %copy.20), channel_id=1, source_target_pairs={{0,8},{8,16},{16,24},{24,0},{1,9},{9,17},{17,25},{25,1},{2,10},{10... | collective-permute-start | bytes 73736 | tf_op jit(solution)/shard_map/ppermute | solution.py:178
  39.3 28.7 %copy-start.9 = (f32[112]{0:T(128)S(1)}, f32[112]{0:T(128)}, u32[]{:S(2)}) copy-start(f32[112]{0:T(128)} %param.10) | copy-start | bytes 1348
  39.3 29.4 %copy-start.10 = (f32[112]{0:T(128)S(1)}, f32[112]{0:T(128)}, u32[]{:S(2)}) copy-start(f32[112]{0:T(128)} %param.11) | copy-start | bytes 1348
  41.9 57.4 %collective-permute-start.1 = (bf16[1,48,256]{2,1,0:T(8,128)(2,1)S(1)}, bf16[1,48,256]{2,1,0:T(8,128)(2,1)S(1)}, u32[]{:S(2)}, u32[]{:S(2)}) collective-permute-start(bf16[1,48,256]{2,1,0:T(8,128)(2,1)S(1)} %copy.21), channel_id=1, source_target_pairs={{8,0},{16,8},{24,16},{0,24},{9,1},{17,9},{25,17},{1,25},{10,2},{18... | collective-permute-start | bytes 73736 | tf_op jit(solution)/shard_map/ppermute | solution.py:179
  99.3 0.6 copy-start.5
  99.3 0.6 copy-start.7
  113.6 10.6 %collective-permute-start.4 = (bf16[1,48,256]{2,1,0:T(8,128)(2,1)S(1)}, bf16[1,48,256]{2,1,0:T(8,128)(2,1)S(1)}, u32[]{:S(2)}, u32[]{:S(2)}) collective-permute-start(bf16[1,48,256]{2,1,0:T(8,128)(2,1)S(1)} %get-tuple-element.12), channel_id=1, source_target_pairs={{0,8},{8,16},{16,24},{24,0},{1,9},{9,17},{17,25},{25,1},{2,10},{10... | collective-permute-start | bytes 73736 | tf_op jit(solution)/shard_map/ppermute | solution.py:178
  115.0 9.1 %collective-permute-start.5 = (bf16[1,48,256]{2,1,0:T(8,128)(2,1)S(1)}, bf16[1,48,256]{2,1,0:T(8,128)(2,1)S(1)}, u32[]{:S(2)}, u32[]{:S(2)}) collective-permute-start(bf16[1,48,256]{2,1,0:T(8,128)(2,1)S(1)} %get-tuple-element.11), channel_id=1, source_target_pairs={{8,0},{16,8},{24,16},{0,24},{9,1},{17,9},{25,17},{1,25},{10,2},{18... | collective-permute-start | bytes 73736 | tf_op jit(solution)/shard_map/ppermute | solution.py:179
  118.0 4.9 %collective-permute-start.6 = (bf16[48,16]{1,0:T(8,128)(2,1)S(1)}, bf16[48,16]{1,0:T(8,128)(2,1)S(1)}, u32[]{:S(2)}, u32[]{:S(2)}) collective-permute-start(bf16[48,16]{1,0:T(8,128)(2,1)S(1)} %bitcast.30), channel_id=1, source_target_pairs={{0,1},{1,2},{2,3},{3,4},{4,5},{5,6},{6,7},{7,0},{8,9},{9,10},{10,1... | collective-permute-start | bytes 4616 | tf_op jit(solution)/shard_map/ppermute | solution.py:180
  118.4 5.1 %collective-permute-start.7 = (bf16[48,16]{1,0:T(8,128)(2,1)S(1)}, bf16[48,16]{1,0:T(8,128)(2,1)S(1)}, u32[]{:S(2)}, u32[]{:S(2)}) collective-permute-start(bf16[48,16]{1,0:T(8,128)(2,1)S(1)} %bitcast.31), channel_id=1, source_target_pairs={{1,0},{2,1},{3,2},{4,3},{5,4},{6,5},{7,6},{0,7},{9,8},{10,9},{11,1... | collective-permute-start | bytes 4616 | tf_op jit(solution)/shard_map/ppermute | solution.py:181
  124.2 0.6 copy-start.6
  124.8 0.6 copy-start.8

commit v2 on v1

--- a/solution.py
+++ b/solution.py
@@ -14,11 +14,14 @@
 VSPEC = pl.BlockSpec(memory_space=pltpu.VMEM)
 
 
-def partial_kernel(chunks, vals_ref, parent_ref, out_ref, onehot, masked):
-    rows, feats, lanes = vals_ref.shape
-    owner = pl.program_id(0)
-
-    @pl.when(owner == 0)
+def partial_kernel(chunks, offset_ref, temp_ref, humid_ref, parent_ref, out_ref, onehot, masked):
+    rows, levels, lanes = temp_ref.shape
+    step = pl.program_id(0)
+    owner = 2 * step + offset_ref[0]
+    data = 2 * levels * chunks
+    row = lax.broadcasted_iota(jnp.int32, (16, lanes), 0)
+
+    @pl.when(step == 0)
     def _():
         lo_iota = lax.broadcasted_iota(jnp.int32, (lanes, lanes), 0)
         for r in range(rows):
@@ -27,32 +30,34 @@
 
     for r in range(rows):
         high = jnp.broadcast_to(parent_ref[r : r + 1, :] // lanes, (16, lanes))
+        part = slice(r * lanes, (r + 1) * lanes)
         for c in range(chunks):
             mask = (high == owner * chunks + c).astype(F32).astype(BF16)
-            for v in range(feats // 16):
-                at = c * feats + v * 16
-                masked[at : at + 16, r * lanes : (r + 1) * lanes] = (
-                    vals_ref[r, v * 16 : (v + 1) * 16, :] * mask
-                )
+            for v in range(levels // 16):
+                src = slice(v * 16, (v + 1) * 16)
+                at = c * 2 * levels + v * 16
+                masked[at : at + 16, part] = temp_ref[r, src, :] * mask
+                masked[at + levels : at + levels + 16, part] = humid_ref[r, src, :] * mask
+        masked[data : data + 16, part] = (high == owner * chunks + row // 2).astype(F32).astype(BF16)
     total = lax.dot_general(
         masked[...], onehot[...], (((1,), (1,)), ((), ())), preferred_element_type=F32
     )
-    out_ref[0] = total.astype(BF16)
-    for c in range(chunks):
-        at = slice((c + 1) * feats - 16, (c + 1) * feats)
-        count = total[at]
-        high = jnp.floor(count * (1.0 / 32.0))
-        row = lax.broadcasted_iota(jnp.int32, count.shape, 0)
-        out_ref[0, at, :] = jnp.where(row == 0, high, count - 32.0 * high).astype(BF16)
-
-
-def radiate_kernel(levels, feats, recv_ref, kabs_ref, planck_ref, top_ref, out_ref, sums, absorb, emit, trans, net, heat):
+    out_ref[0, :data, :] = total[:data].astype(out_ref.dtype)
+    count = total[data:]
+    high = jnp.floor(count * (1.0 / 32.0))
+    out_ref[0, data:, :] = jnp.where(row % 2 == 0, high, count - 32.0 * high).astype(out_ref.dtype)
+
+
+def radiate_kernel(levels, feats, recv_ref, kabs_in, planck_ref, top_ref, out_ref, kabs_ref, sums, absorb, emit, trans, net, heat):
     tiles = recv_ref.shape[0]
     lanes = recv_ref.shape[2]
     chunks = recv_ref.shape[1] // feats
-    octets = kabs_ref.shape[1] // 8
+    octets = kabs_in.shape[0] // 8
     group = octets // 2 if octets % 2 == 0 else octets
     width = 128
+    data = chunks * feats
+    for k in range(levels):
+        kabs_ref[k] = jnp.broadcast_to(kabs_in[:, k : k + 1], kabs_ref.shape[1:])
 
     def add(i, carry):
         at = pl.ds(pl.multiple_of(i * 16, 16), 16)
@@ -62,11 +67,11 @@
         sums[at, :] = acc
         return carry
 
-    lax.fori_loop(0, chunks * feats // 16, add, 0)
+    lax.fori_loop(0, data // 16 + 1, add, 0)
     for c in range(chunks):
         base = c * feats
-        cnt = sums[base + 2 * levels : base + 2 * levels + 1, :] * 32.0
-        cnt = cnt + sums[base + 2 * levels + 1 : base + 2 * levels + 2, :]
+        cnt = sums[data + 2 * c : data + 2 * c + 1, :] * 32.0
+        cnt = cnt + sums[data + 2 * c + 1 : data + 2 * c + 2, :]
         cnt = jnp.maximum(cnt, 1.0)
         for j in range(lanes // width):
             part = slice(j * width, (j + 1) * width)
@@ -82,8 +87,8 @@
     def column(ct, carry):
         for half in range(octets // group):
             gs = [(half * group + p) * 8 for p in range(group)]
-            planck = [planck_ref[g : g + 8, :] for g in gs]
-            down = [top_ref[g : g + 8, :] for g in gs]
+            planck = [jnp.broadcast_to(planck_ref[g : g + 8, :], (8, width)) for g in gs]
+            down = [jnp.broadcast_to(top_ref[g : g + 8, :], (8, width)) for g in gs]
             if half == 0:
                 before = sum(down[1:], down[0])
                 net[0] = before
@@ -187,34 +192,49 @@
     tiles = lax.axis_size("tile")
     owned = rows * lanes // 4
     chunks = owned // lanes
-    feats = 2 * levels + 16
+    feats = 2 * levels
     gpts = kabs.shape[0]
     params = pltpu.CompilerParams(vmem_limit_bytes=VMEM_LIMIT)
 
     x = jnp.transpose(temp, (1, 0, 2))
     h = jnp.transpose(humid, (1, 0, 2))
-    ones = jnp.ones((rows, 16, lanes), BF16)
-    vals = jnp.concatenate([x, h, ones], 1)
-    partial = pl.pallas_call(
-        functools.partial(partial_kernel, chunks),
-        out_shape=jax.ShapeDtypeStruct((tiles, chunks * feats, lanes), BF16),
-        grid=(tiles,),
-        in_specs=[
-            pl.BlockSpec((rows, feats, lanes), lambda i: (0, 0, 0)),
-            pl.BlockSpec((rows, lanes), lambda i: (0, 0)),
-        ],
-        out_specs=pl.BlockSpec((1, chunks * feats, lanes), lambda i: (i, 0, 0)),
-        scratch_shapes=[
-            pltpu.VMEM((lanes, rows * lanes), BF16),
-            pltpu.VMEM((chunks * feats, rows * lanes), BF16),
-        ],
-        compiler_params=params,
-    )(vals, parent)
-    recv = lax.all_to_all(partial, "tile", split_axis=0, concat_axis=0, tiled=True)
-
-    kb = jnp.broadcast_to(jnp.transpose(kabs)[:, :, None], (levels, gpts, 128))
-    pb = jnp.broadcast_to(planck[:, None], (gpts, 128))
-    tb = jnp.broadcast_to(top_flux[:, None], (gpts, 128))
+    size = chunks * feats + 16
+    core = lax.rem(lax.axis_index("tile"), 2)
+    half = tiles // 2
+
+    def partial_sums(offset, dtype):
+        return pl.pallas_call(
+            functools.partial(partial_kernel, chunks),
+            out_shape=jax.ShapeDtypeStruct((half, size, lanes), dtype),
+            grid=(half,),
+            in_specs=[
+                pl.BlockSpec(memory_space=pltpu.SMEM),
+                pl.BlockSpec((rows, levels, lanes), lambda i: (0, 0, 0)),
+                pl.BlockSpec((rows, levels, lanes), lambda i: (0, 0, 0)),
+                pl.BlockSpec((rows, lanes), lambda i: (0, 0)),
+            ],
+            out_specs=pl.BlockSpec((1, size, lanes), lambda i: (i, 0, 0)),
+            scratch_shapes=[
+                pltpu.VMEM((lanes, rows * lanes), BF16),
+                pltpu.VMEM((size, rows * lanes), BF16),
+            ],
+            compiler_params=params,
+            cost_estimate=pl.CostEstimate(
+                flops=2 * half * size * rows * lanes * lanes,
+                bytes_accessed=4 * half * size * lanes,
+                transcendentals=0,
+            ),
+        )(offset.reshape(1).astype(jnp.int32), x, h, parent)
+
+    theirs = partial_sums(1 - core, BF16)
+    given = lax.ppermute(theirs, "tile", [(i, i ^ 1) for i in range(tiles)])
+    mine = partial_sums(core, F32)
+    partial = (mine + given.astype(F32)).astype(BF16)
+    groups = [list(range(c, tiles, 2)) for c in range(2)]
+    recv = lax.all_to_all(
+        partial, "tile", split_axis=0, concat_axis=0, tiled=True, axis_index_groups=groups
+    )
+
     ctiles = owned // 128
     octets = gpts // 8
     group = octets // 2 if octets % 2 == 0 else octets
@@ -224,7 +244,8 @@
         in_specs=[VSPEC] * 4,
         out_specs=VSPEC,
         scratch_shapes=[
-            pltpu.VMEM((chunks * feats, lanes), F32),
+            pltpu.VMEM((levels, gpts, 128), F32),
+            pltpu.VMEM((size, lanes), F32),
             pltpu.VMEM((ctiles, levels, 128), F32),
             pltpu.VMEM((ctiles, levels, 128), F32),
             pltpu.VMEM((levels, group, 8, 128), F32),
@@ -232,7 +253,7 @@
             pltpu.VMEM((ctiles, levels, 128), F32),
         ],
         compiler_params=params,
-    )(recv, kb, pb, tb)
+    )(recv, kabs, planck[:, None], top_flux[:, None])
     tables = lax.all_gather(table, "tile", axis=0)
 
     second = pl.pallas_call(

time: 130 us -> 110 us (0.85)
  waiting for transfers between devices: 22.5 us -> 0.99 us
    ppermute x2, waiting for transfers between devices: 14.4 us -> 0.97 us  [halos(): lf = lax.ppermute(jnp.transpose(x[:, :, -1]), 'tile', ahead(t)).astype(F32)]
    all_to_all x1, waiting for transfers between devices: 8.1 us -> 0.01 us  [on_device(): lax.all_to_all(partial, 'tile', split_axis=0, concat_axis=0, tiled=True,...]
    convert_element_type x0 -> x1, other arithmetic: none -> 2.57 us  [on_device(): partial = (mine + given.astype(F32)).astype(BF16)]
    broadcast_in_dim x4 -> x2, local copies, waits for them, and re-layouts: 3.37 us -> 1.44 us  [the longest x1 0.72 us: on_device(): top_flux[:, None]]
    pallas_call x1 -> x2, Pallas kernels: 11.7 us -> 13 us  [partial_sums(): pl.pallas_call(functools.partial(partial_kernel, chunks), out_shape=jax.S...]
    unnamed x26 -> x23, local copies, waits for them, and re-layouts: 7.29 us -> 8.11 us
  transfers between devices with their start and end apart: 9 -> 10, of which waited for: 3 -> 1; matrix products, arithmetic and copies ran while one was open for 17% -> 19% of each run, Pallas kernels for 10% -> 17%
where the time goes in v2:
time: 110 us; the launch traced here: 109 us
  Pallas kernels  40.7 us (37%)
  local copies, waits for them, and re-layouts  26.5 us (24%)
  starting transfers between devices  19.5 us (18%)
  blocking collectives  16.8 us (15%)
  other arithmetic  4.98 us (5%)
    all_gather x1, blocking collectives, on_device(): tables = lax.all_gather(table, 'tile', axis=0)  16.8 us
    pallas_call x2, Pallas kernels, partial_sums(): pl.pallas_call(functools.partial(partial_kernel, chunks), out_shape=jax.S...  13 us
    pallas_call x1, Pallas kernels, on_device(): pl.pallas_call(functools.partial(gather_kernel, levels), out_shape=jax.Sh...  12.8 us
    pallas_call x1, Pallas kernels, on_device(): pl.pallas_call(functools.partial(radiate_kernel, levels, feats), out_shap...  12.5 us
    unnamed x23, local copies, waits for them, and re-layouts  8.11 us
    slice x3, local copies, waits for them, and re-layouts, halos(): dn = lax.ppermute(x[:1], 'grp', back(g))  7.35 us
    ppermute x2, starting transfers between devices, halos(): rt = lax.ppermute(jnp.transpose(x[:, :, 0]), 'tile', back(t)).astype(F32)  6.87 us
    all_to_all x1, starting transfers between devices, on_device(): lax.all_to_all(partial, 'tile', split_axis=0, concat_axis=0, tiled=True,...  5.86 us
  transfers between devices with their start and end apart: 10, of which 1 were waited for; matrix products, arithmetic and copies ran while one was open for 19% of the time, Pallas kernels for 17%

profile of v2, /device:TPU:0, one launch (start us, length us, event | category | flops | bytes accessed | tf_op | source)
XLA Modules:
  0.0 109.5 jit_solution(12303522389427395330)
XLA Ops:
  0.0 1.9 %copy.37 = bf16[48,16,256]{2,0,1:T(8,128)(2,1)} copy(bf16[48,16,256]{2,1,0:T(8,128)(2,1)} %param.7) | data formatting | bytes 786432 | tf_op args[1]
  1.9 1.9 %copy.22.temp_ref = bf16[16,48,256]{2,1,0:T(8,128)(2,1)} copy(bf16[16,48,256]{2,0,1:T(8,128)(2,1)} %bitcast.28) | data formatting | bytes 786432 | tf_op jit(solution)/shard_map/transpose | solution.py:199
  3.7 6.4 %shard_map.65 = bf16[4,400,256]{2,1,0:T(8,128)(2,1)} custom-call(s32[1]{0:T(128)} %bitcast.4.offset_ref, bf16[16,48,256]{2,1,0:T(8,128)(2,1)} %copy.22.temp_ref, bf16[16,48,256]{2,1,0:T(8,128)(2,1)} %bitcast.30, s32[16,256]{1,0:T(8,128)} %parent_ref.5), custom_call_target="tpu_custom_call" | custom-call | flops 3355443200 | bytes 1638400 | tf_op jit(solution)/shard_map/pallas_call | solution.py:206
  10.2 0.5 collective-permute-start
  10.7 6.5 %shard_map.64 = f32[4,400,256]{2,1,0:T(8,128)} custom-call(s32[1]{0:T(128)} %bitcast.offset_ref, bf16[16,48,256]{2,1,0:T(8,128)(2,1)} %copy.22.temp_ref, bf16[16,48,256]{2,1,0:T(8,128)(2,1)} %bitcast.31, s32[16,256]{1,0:T(8,128)} %parent_ref.5), custom_call_target="tpu_custom_call" | custom-call | flops 3355443200 | bytes 1638400 | tf_op jit(solution)/shard_map/pallas_call | solution.py:206
  17.2 0.0 copy-start.1
  17.2 0.0 collective-permute-done
  17.2 2.6 %add_convert_fusion = bf16[4,400,256]{2,1,0:T(8,128)(2,1)} fusion(f32[4,400,256]{2,1,0:T(8,128)} %shard_map.64, bf16[4,400,256]{2,1,0:T(8,128)(2,1)S(1)} %collective-permute-done), kind=kLoop, calls=%fused_computation | loop fusion | flops 1228800 | bytes 3276800 | tf_op jit(solution)/shard_map/convert_element_type | solution.py:232
  19.8 5.9 %all-to-all-start = ((bf16[4,400,256]{2,1,0:T(8,128)(2,1)}), bf16[4,400,256]{2,1,0:T(8,128)(2,1)}, u32[]{:S(2)}, u32[]{:S(2)}) async-start(bf16[4,400,256]{2,1,0:T(8,128)(2,1)} %add_convert_fusion), calls=%async_computation | async-start | bytes 1638400 | tf_op jit(solution)/shard_map/all_to_all | solution.py:234
  25.6 0.0 copy-done.1
  25.6 2.9 %copy.20 = bf16[48,16,256]{1,0,2:T(8,128)(2,1)S(1)} copy(bf16[48,16,256]{2,1,0:T(8,128)(2,1)S(1)} %copy-done.1) | data formatting | bytes 786432 | tf_op args[0]
  28.6 0.3 collective-permute-start.3
  28.9 3.3 %collective-permute-start.4 = (bf16[48,16]{1,0:T(8,128)(2,1)S(1)}, bf16[48,16]{1,0:T(8,128)(2,1)S(1)}, u32[]{:S(2)}, u32[]{:S(2)}) collective-permute-start(bf16[48,16]{1,0:T(8,128)(2,1)S(1)} %get-tuple-element.5), channel_id=1, source_target_pairs={{1,0},{2,1},{3,2},{4,3},{5,4},{6,5},{7,6},{0,7},{9,8},{10,9},{11,1... | collective-permute-start | bytes 4616 | tf_op jit(solution)/shard_map/ppermute | solution.py:186
  32.2 4.0 %fusion = (bf16[1,48,256]{0,1,2:T(8,128)(2,1)}, bf16[1,48,256]{0,1,2:T(8,128)(2,1)}) fusion(bf16[16,48,256]{0,1,2:T(8,128)(2,1)S(1)} %bitcast.26), kind=kLoop, calls=%fused_computation.4 | loop fusion | bytes 98304 | tf_op jit(solution)/shard_map/slice | solution.py:184
  36.2 0.0 copy-start
  36.2 0.0 copy-start.6
  36.2 0.0 copy-start.7
  36.2 0.0 copy-start.8
  36.2 4.7 %copy.27 = bf16[1,48,256]{2,1,0:T(8,128)(2,1)S(1)} copy(bf16[1,48,256]{0,1,2:T(8,128)(2,1)} %get-tuple-element.8) | data formatting | bytes 49152 | tf_op jit(solution)/shard_map/slice | solution.py:183
  40.9 1.5 %collective-permute-start.1 = (bf16[1,48,256]{2,1,0:T(8,128)(2,1)S(1)}, bf16[1,48,256]{2,1,0:T(8,128)(2,1)S(1)}, u32[]{:S(2)}, u32[]{:S(2)}) collective-permute-start(bf16[1,48,256]{2,1,0:T(8,128)(2,1)S(1)} %copy.27), channel_id=1, source_target_pairs={{0,8},{8,16},{16,24},{24,0},{1,9},{9,17},{17,25},{25,1},{2,10},{10... | collective-permute-start | bytes 73736 | tf_op jit(solution)/shard_map/ppermute | solution.py:183
  42.5 0.0 copy-done
  42.5 2.6 %copy.28 = bf16[1,48,256]{2,1,0:T(8,128)(2,1)S(1)} copy(bf16[1,48,256]{0,1,2:T(8,128)(2,1)S(1)} %copy-done) | data formatting | bytes 49152 | tf_op jit(solution)/shard_map/slice | solution.py:184
  45.0 1.5 %collective-permute-start.2 = (bf16[1,48,256]{2,1,0:T(8,128)(2,1)S(1)}, bf16[1,48,256]{2,1,0:T(8,128)(2,1)S(1)}, u32[]{:S(2)}, u32[]{:S(2)}) collective-permute-start(bf16[1,48,256]{2,1,0:T(8,128)(2,1)S(1)} %copy.28), channel_id=1, source_target_pairs={{8,0},{16,8},{24,16},{0,24},{9,1},{17,9},{25,17},{1,25},{10,2},{18... | collective-permute-start | bytes 73736 | tf_op jit(solution)/shard_map/ppermute | solution.py:184
  46.5 0.0 copy-done.6
  46.5 0.7 copy.24.kabs_in
  47.2 0.0 copy-done.7
  47.2 0.7 copy.25.planck_ref
  47.9 0.0 copy-done.8
  47.9 0.7 copy.26.top_ref
  48.7 0.0 collective-permute-done.3
  48.7 0.6 convert_element_type.20.lf_ref
  49.3 0.0 collective-permute-done.4
  49.3 0.6 convert_element_type.21.rt_ref
  49.9 0.0 all-to-all-done.recv_ref
  49.9 12.5 %shard_map.66 = bf16[192,256]{1,0:T(8,128)(2,1)} custom-call(bf16[4,400,256]{2,1,0:T(8,128)(2,1)} %all-to-all-done.recv_ref, f32[112,48]{1,0:T(8,128)} %copy.24.kabs_in, f32[112,1]{1,0:T(8,128)} %copy.25.planck_ref, f32[112,1]{1,0:T(8,128)} %copy.26.top_ref), custom_call_target="tpu_custom_call" | custom-call | tf_op jit(solution)/shard_map/pallas_call | solution.py:241
  62.4 16.8 %all-gather = bf16[1536,256]{1,0:T(8,128)(2,1)} all-gather(bf16[192,256]{1,0:T(8,128)(2,1)} %shard_map.66), channel_id=2, replica_groups=mesh['grp'=4,'tile'=8] {'tile'}, dimensions={0}, use_global_device_ids=true | all-gather | bytes 884736 | tf_op jit(solution)/shard_map/all_gather | solution.py:257
  79.2 0.0 collective-permute-done.1.up_ref
  79.2 0.0 copy-start.2
  79.2 0.0 collective-permute-done.2.dn_ref
  79.2 0.0 copy-start.4
  79.3 0.6 copy-done.2
  79.8 0.0 copy-done.4
  79.9 12.8 %shard_map.67.x_ref = bf16[16,48,256]{2,1,0:T(8,128)(2,1)} custom-call(bf16[8,192,256]{2,1,0:T(8,128)(2,1)} %bitcast.27, s32[16,256]{1,0:T(8,128)} %parent_ref.5, bf16[16,48,256]{2,1,0:T(8,128)(2,1)} %copy.22.temp_ref, bf16[16,48,256]{2,1,0:T(8,128)(2,1)} %bitcast.32, bf16[1,48,256]{2,1,0:T(8,128)(2,1)} %copy-done.2, bf16[1,48,256]{2,1,0:T(8,128)(2,1)} %copy-done.4, ...), custom_call_target="tpu_custom_call" | custom-call | tf_op jit(solution)/shard_map/pallas_call | solution.py:259
  92.7 0.8 fusion.2
  93.5 0.5 collective-permute-start.5
  94.0 2.4 %collective-permute-start.6 = (bf16[1,48,256]{2,1,0:T(8,128)(2,1)S(1)}, bf16[1,48,256]{2,1,0:T(8,128)(2,1)S(1)}, u32[]{:S(2)}, u32[]{:S(2)}) collective-permute-start(bf16[1,48,256]{2,1,0:T(8,128)(2,1)S(1)} %get-tuple-element.11), channel_id=1, source_target_pairs={{8,0},{16,8},{24,16},{0,24},{9,1},{17,9},{25,17},{1,25},{10,2},{18... | collective-permute-start | bytes 73736 | tf_op jit(solution)/shard_map/ppermute | solution.py:184
  96.4 1.1 %fusion.1 = (bf16[16,48,1]{2,1,0:T(8,128)(2,1)S(1)}, bf16[16,48,1]{2,1,0:T(8,128)(2,1)S(1)}) fusion(bf16[16,48,256]{2,1,0:T(8,128)(2,1)} %shard_map.67.x_ref), kind=kLoop, calls=%fused_computation.5 | loop fusion | bytes 6144 | tf_op jit(solution)/shard_map/slice | solution.py:186
  97.5 0.4 copy.34
  97.9 0.0 collective-permute-start.7
  97.9 0.4 copy.35
  98.3 3.5 %collective-permute-start.8 = (bf16[48,16]{1,0:T(8,128)(2,1)S(1)}, bf16[48,16]{1,0:T(8,128)(2,1)S(1)}, u32[]{:S(2)}, u32[]{:S(2)}) collective-permute-start(bf16[48,16]{1,0:T(8,128)(2,1)S(1)} %bitcast.34), channel_id=1, source_target_pairs={{1,0},{2,1},{3,2},{4,3},{5,4},{6,5},{7,6},{0,7},{9,8},{10,9},{11,1... | collective-permute-start | bytes 4616 | tf_op jit(solution)/shard_map/ppermute | solution.py:186
  101.9 1.0 collective-permute-done.7
  102.8 0.6 convert_element_type.22.lf_ref
  103.4 0.0 collective-permute-done.8
  103.5 0.6 convert_element_type.23.rt_ref
  104.1 0.0 collective-permute-done.5.up_ref
  104.1 0.0 copy-start.3
  104.1 0.0 collective-permute-done.6.dn_ref
  104.1 0.6 copy-done.3
  104.7 0.0 copy-start.5
  104.7 0.6 copy-done.5
  105.3 2.3 %shard_map.68 = bf16[16,48,256]{2,1,0:T(8,128)(2,1)} custom-call(bf16[16,48,256]{2,1,0:T(8,128)(2,1)} %shard_map.67.x_ref, bf16[1,48,256]{2,1,0:T(8,128)(2,1)} %copy-done.3, bf16[1,48,256]{2,1,0:T(8,128)(2,1)} %copy-done.5, f32[48,16]{1,0:T(8,128)} %convert_element_type.22.lf_ref, f32[48,16]{1,0:T(8,128)} %convert_element_type.23.rt_ref), custom_call_target="tpu_custom_call" | custom-call | tf_op jit(solution)/shard_map/pallas_call | solution.py:266
  107.6 1.9 %copy.32 = bf16[48,16,256]{2,1,0:T(8,128)(2,1)} copy(bf16[48,16,256]{2,0,1:T(8,128)(2,1)} %bitcast.29) | data formatting | bytes 786432 | tf_op jit(solution)/shard_map/transpose | solution.py:273
  (1 shorter events, 0.0 us)
Async XLA Ops:
  10.2 7.0 %collective-permute-start = (bf16[4,400,256]{2,1,0:T(8,128)(2,1)}, bf16[4,400,256]{2,1,0:T(8,128)(2,1)S(1)}, u32[]{:S(2)}, u32[]{:S(2)}) collective-permute-start(bf16[4,400,256]{2,1,0:T(8,128)(2,1)} %shard_map.65), channel_id=1, source_target_pairs={{0,1},{1,0},{2,3},{3,2},{4,5},{5,4},{6,7},{7,6},{8,9},{9,8},{10,11... | collective-permute-start | bytes 2457608 | tf_op jit(solution)/shard_map/ppermute | solution.py:230
  17.2 8.4 %copy-start.1 = (bf16[48,16,256]{2,1,0:T(8,128)(2,1)S(1)}, bf16[48,16,256]{2,1,0:T(8,128)(2,1)}, u32[]{:S(2)}) copy-start(bf16[48,16,256]{2,1,0:T(8,128)(2,1)} %param.6) | copy-start | bytes 1179652
  19.8 30.1 %all-to-all-start = ((bf16[4,400,256]{2,1,0:T(8,128)(2,1)}), bf16[4,400,256]{2,1,0:T(8,128)(2,1)}, u32[]{:S(2)}, u32[]{:S(2)}) async-start(bf16[4,400,256]{2,1,0:T(8,128)(2,1)} %add_convert_fusion), calls=%async_computation | async-start | bytes 1638400 | tf_op jit(solution)/shard_map/all_to_all | solution.py:234
  28.6 20.1 %collective-permute-start.3 = (bf16[48,16]{1,0:T(8,128)(2,1)S(1)}, bf16[48,16]{1,0:T(8,128)(2,1)S(1)}, u32[]{:S(2)}, u32[]{:S(2)}) collective-permute-start(bf16[48,16]{1,0:T(8,128)(2,1)S(1)} %get-tuple-element.6), channel_id=1, source_target_pairs={{0,1},{1,2},{2,3},{3,4},{4,5},{5,6},{6,7},{7,0},{8,9},{9,10},{10,1... | collective-permute-start | bytes 4616 | tf_op jit(solution)/shard_map/ppermute | solution.py:185
  28.9 20.4 %collective-permute-start.4 = (bf16[48,16]{1,0:T(8,128)(2,1)S(1)}, bf16[48,16]{1,0:T(8,128)(2,1)S(1)}, u32[]{:S(2)}, u32[]{:S(2)}) collective-permute-start(bf16[48,16]{1,0:T(8,128)(2,1)S(1)} %get-tuple-element.5), channel_id=1, source_target_pairs={{1,0},{2,1},{3,2},{4,3},{5,4},{6,5},{7,6},{0,7},{9,8},{10,9},{11,1... | collective-permute-start | bytes 4616 | tf_op jit(solution)/shard_map/ppermute | solution.py:186
  36.2 6.3 %copy-start = (bf16[1,48,256]{0,1,2:T(8,128)(2,1)S(1)}, bf16[1,48,256]{0,1,2:T(8,128)(2,1)}, u32[]{:S(2)}) copy-start(bf16[1,48,256]{0,1,2:T(8,128)(2,1)} %get-tuple-element.7) | copy-start | bytes 73732
  36.2 10.3 %copy-start.6 = (f32[112,48]{0,1:T(8,128)S(1)}, f32[112,48]{0,1:T(8,128)}, u32[]{:S(2)}) copy-start(f32[112,48]{0,1:T(8,128)} %param.9) | copy-start | bytes 64516
  36.2 11.0 %copy-start.7 = (f32[112]{0:T(128)S(1)}, f32[112]{0:T(128)}, u32[]{:S(2)}) copy-start(f32[112]{0:T(128)} %param.10) | copy-start | bytes 1348
  36.2 11.7 %copy-start.8 = (f32[112]{0:T(128)S(1)}, f32[112]{0:T(128)}, u32[]{:S(2)}) copy-start(f32[112]{0:T(128)} %param.11) | copy-start | bytes 1348
  40.9 38.3 %collective-permute-start.1 = (bf16[1,48,256]{2,1,0:T(8,128)(2,1)S(1)}, bf16[1,48,256]{2,1,0:T(8,128)(2,1)S(1)}, u32[]{:S(2)}, u32[]{:S(2)}) collective-permute-start(bf16[1,48,256]{2,1,0:T(8,128)(2,1)S(1)} %copy.27), channel_id=1, source_target_pairs={{0,8},{8,16},{16,24},{24,0},{1,9},{9,17},{17,25},{25,1},{2,10},{10... | collective-permute-start | bytes 73736 | tf_op jit(solution)/shard_map/ppermute | solution.py:183
  45.0 34.2 %collective-permute-start.2 = (bf16[1,48,256]{2,1,0:T(8,128)(2,1)S(1)}, bf16[1,48,256]{2,1,0:T(8,128)(2,1)S(1)}, u32[]{:S(2)}, u32[]{:S(2)}) collective-permute-start(bf16[1,48,256]{2,1,0:T(8,128)(2,1)S(1)} %copy.28), channel_id=1, source_target_pairs={{8,0},{16,8},{24,16},{0,24},{9,1},{17,9},{25,17},{1,25},{10,2},{18... | collective-permute-start | bytes 73736 | tf_op jit(solution)/shard_map/ppermute | solution.py:184
  79.2 0.6 copy-start.2
  79.2 0.6 copy-start.4
  93.5 10.6 %collective-permute-start.5 = (bf16[1,48,256]{2,1,0:T(8,128)(2,1)S(1)}, bf16[1,48,256]{2,1,0:T(8,128)(2,1)S(1)}, u32[]{:S(2)}, u32[]{:S(2)}) collective-permute-start(bf16[1,48,256]{2,1,0:T(8,128)(2,1)S(1)} %get-tuple-element.12), channel_id=1, source_target_pairs={{0,8},{8,16},{16,24},{24,0},{1,9},{9,17},{17,25},{25,1},{2,10},{10... | collective-permute-start | bytes 73736 | tf_op jit(solution)/shard_map/ppermute | solution.py:183
  94.0 10.1 %collective-permute-start.6 = (bf16[1,48,256]{2,1,0:T(8,128)(2,1)S(1)}, bf16[1,48,256]{2,1,0:T(8,128)(2,1)S(1)}, u32[]{:S(2)}, u32[]{:S(2)}) collective-permute-start(bf16[1,48,256]{2,1,0:T(8,128)(2,1)S(1)} %get-tuple-element.11), channel_id=1, source_target_pairs={{8,0},{16,8},{24,16},{0,24},{9,1},{17,9},{25,17},{1,25},{10,2},{18... | collective-permute-start | bytes 73736 | tf_op jit(solution)/shard_map/ppermute | solution.py:184
  97.9 4.9 %collective-permute-start.7 = (bf16[48,16]{1,0:T(8,128)(2,1)S(1)}, bf16[48,16]{1,0:T(8,128)(2,1)S(1)}, u32[]{:S(2)}, u32[]{:S(2)}) collective-permute-start(bf16[48,16]{1,0:T(8,128)(2,1)S(1)} %bitcast.33), channel_id=1, source_target_pairs={{0,1},{1,2},{2,3},{3,4},{4,5},{5,6},{6,7},{7,0},{8,9},{9,10},{10,1... | collective-permute-start | bytes 4616 | tf_op jit(solution)/shard_map/ppermute | solution.py:185
  98.3 5.1 %collective-permute-start.8 = (bf16[48,16]{1,0:T(8,128)(2,1)S(1)}, bf16[48,16]{1,0:T(8,128)(2,1)S(1)}, u32[]{:S(2)}, u32[]{:S(2)}) collective-permute-start(bf16[48,16]{1,0:T(8,128)(2,1)S(1)} %bitcast.34), channel_id=1, source_target_pairs={{1,0},{2,1},{3,2},{4,3},{5,4},{6,5},{7,6},{0,7},{9,8},{10,9},{11,1... | collective-permute-start | bytes 4616 | tf_op jit(solution)/shard_map/ppermute | solution.py:186
  104.1 0.6 copy-start.3
  104.7 0.6 copy-start.5
